TPU v7x, 128 devices: a whole 4x4x4 slice. The times are simulated.
128 devices in a mesh: cfg: 2 (over z_lo), req: 8 (over z_hi, x), seq: 8 (over y, core).
Axes of the slice: x: 4, y: 4, z: 4 (z_hi: 2, z_lo: 2; z = z_hi * 2 + z_lo), core: 2. Of those that a mesh axis runs over, the one named last changes fastest.
Arguments:
- img_state: bfloat16 [2, 16, 1024, 1536], P('cfg', 'req', 'seq'), may hold values from -6 to 6
- txt_state: bfloat16 [2, 16, 192, 1536], P('cfg', 'req', 'seq'), may hold values from -6 to 6
- cond_vec: float32 [2, 16, 1536], P('cfg'), may hold values from -6 to 6
- text_len: int32 [2, 16], P('cfg', 'req'), may hold values from 38 to 154, as said below
- latent: float32 [16, 1024, 64], P('req', 'seq', 'cfg'), may hold values from -6 to 6
- w_mod: bfloat16 [15360, 1536], P(('req', 'seq')), may hold values from -0.15625 to 0.15625
- w_qkv_img: bfloat16 [3, 1536, 1536], P(None, 'seq')
- w_qkv_txt: bfloat16 [3, 1536, 1536], P(None, 'seq')
- w_attn_out: bfloat16 [1536, 1536], P('seq'), may hold values from -2 to 2
- w_up: bfloat16 [6144, 1536], P(('cfg', 'req', 'seq')), may hold values from -0.15625 to 0.15625
- w_down: bfloat16 [6144, 1536], P(('cfg', 'req', 'seq')), may hold values from -0.078125 to 0.078125
- w_final: bfloat16 [1536, 64], replicated, may hold values from -0.078125 to 0.078125
Outputs:
- velocity: float32 [16, 1024, 64], P('req', 'seq', 'cfg')
- latent_next: float32 [16, 1024, 64], P('req', 'seq', 'cfg')
Inputs may be any that keep to these rules, and one draw needn't show every extreme that they name: Text slot t of prompt p in branch c is live when t < text_len[c, p]; every draw has a length equal to 154.
All inputs are finite; a program needn't handle non-finite values.
Results may differ from a plain program's by a relative error of at most 0.02.
Values may be sent and summed in bfloat16 or wider, within the bound.
No kernel may reach another device: no remote copies, remote signals or barrier semaphores. Data moves between devices by JAX's collectives and lax.ppermute only.
A program may use at most 128 MiB of HBM per device.

v0:
```python
import jax
import jax.numpy as jnp
from jax import lax
from jax.sharding import PartitionSpec as P

HEAD = 64


def partner_2(shard, axis, apart):
    return lax.ppermute(shard, axis, [(i, i ^ 1 << apart) for i in range(lax.axis_size(axis))])


def layer_norm(value):
    mean = jnp.mean(value, axis=-1, keepdims=True)
    centered = value - mean
    spread = jnp.mean(centered * centered, axis=-1, keepdims=True)
    return centered * lax.rsqrt(spread + 1e-06)


def mlp_term(rows_in, up_block, down_block):
    inner = lax.dot_general(
        rows_in, up_block, (((1,), (1,)), ((), ())), preferred_element_type=jnp.float32
    )
    hidden = jax.nn.gelu(inner, approximate=True).astype(jnp.bfloat16)
    return jnp.dot(hidden, down_block, preferred_element_type=jnp.float32)


def local(
    img_state,
    txt_state,
    cond_vec,
    text_len,
    latent,
    w_mod,
    w_qkv_img,
    w_qkv_txt,
    w_attn_out,
    w_up,
    w_down,
    w_final,
):
    prompts_dev = img_state.shape[1]
    img_rows = img_state.shape[2]
    width = img_state.shape[3]
    cond_act = jax.nn.silu(cond_vec[0]).astype(jnp.bfloat16)
    mod_part = lax.dot_general(
        cond_act, w_mod, (((1,), (1,)), ((), ())), preferred_element_type=jnp.float32
    )
    mod_all = lax.all_gather(mod_part, ("req", "seq"), axis=1, tiled=True)
    mine = lax.dynamic_slice_in_dim(mod_all, lax.axis_index("req") * prompts_dev, prompts_dev, 0)
    parts = mine.reshape(prompts_dev, 10, 1, width)
    resid = img_state[0].astype(jnp.float32)
    a_img = (layer_norm(resid) * (1.0 + parts[:, 1]) + parts[:, 0]).astype(jnp.bfloat16)
    a_txt = (
        layer_norm(txt_state[0].astype(jnp.float32)) * (1.0 + parts[:, 7]) + parts[:, 6]
    ).astype(jnp.bfloat16)
    full_img, full_txt = (
        lax.all_gather(a_img, "seq", axis=1, tiled=True),
        lax.all_gather(a_txt, "seq", axis=1, tiled=True),
    )
    proj_img = jnp.einsum(
        "pnd,jed->jpne", full_img, w_qkv_img, preferred_element_type=jnp.float32
    ).astype(jnp.bfloat16)
    proj_txt = jnp.einsum(
        "pnd,jed->jpne", full_txt, w_qkv_txt, preferred_element_type=jnp.float32
    ).astype(jnp.bfloat16)
    total_img = full_img.shape[1]
    local_width = w_qkv_img.shape[1]
    heads_local = local_width // HEAD
    key_heads = jnp.concatenate([proj_img[1], proj_txt[1]], axis=1).reshape(
        prompts_dev, -1, heads_local, HEAD
    )
    value_heads = jnp.concatenate([proj_img[2], proj_txt[2]], axis=1).reshape(
        prompts_dev, -1, heads_local, HEAD
    )
    live = jnp.arange(key_heads.shape[1])[None, :] < (total_img + text_len[0])[:, None]
    block = min(512, total_img)
    queries = proj_img[0].reshape(prompts_dev, total_img // block, block, heads_local, HEAD)

    def attend(query):
        scores = jnp.einsum(
            "pqhe,pkhe->phqk", query, key_heads, preferred_element_type=jnp.float32
        ) * HEAD ** (-0.5)
        scores = jnp.where(live[:, None, None, :], scores, -1e30)
        probs = jax.nn.softmax(scores, axis=-1).astype(jnp.bfloat16)
        return jnp.einsum(
            "phqk,pkhe->pqhe", probs, value_heads, preferred_element_type=jnp.float32
        ).astype(jnp.bfloat16)

    attended = lax.map(attend, jnp.moveaxis(queries, 1, 0))
    attended = jnp.moveaxis(attended, 0, 1).reshape(prompts_dev, total_img, local_width)
    proj = jnp.swapaxes(
        lax.psum_scatter(
            jnp.einsum(
                "pnh,hd->npd", attended, w_attn_out, preferred_element_type=jnp.float32
            ).astype(jnp.bfloat16),
            "seq",
            scatter_dimension=0,
            tiled=True,
        ).astype(jnp.float32),
        0,
        1,
    )
    resid_one = (resid + parts[:, 2] * proj).astype(jnp.bfloat16)
    normed = (layer_norm(resid_one.astype(jnp.float32)) * (1.0 + parts[:, 4]) + parts[:, 3]).astype(
        jnp.bfloat16
    )
    own_rows = normed.reshape(prompts_dev * img_rows, width)
    both = lax.all_gather(own_rows, "cfg", axis=0, tiled=True)
    partial_out = mlp_term(
        both,
        lax.all_gather(w_up, ("req", "seq"), axis=0, tiled=True),
        lax.all_gather(w_down, ("req", "seq"), axis=0, tiled=True),
    )
    mlp_out = lax.psum_scatter(
        partial_out.astype(jnp.bfloat16), "cfg", scatter_dimension=0, tiled=True
    ).astype(jnp.float32)
    mlp_out = mlp_out.reshape(prompts_dev, img_rows, width)
    resid_two = resid_one.astype(jnp.float32) + parts[:, 5] * mlp_out
    final_in = (layer_norm(resid_two) * (1.0 + parts[:, 9]) + parts[:, 8]).astype(jnp.bfloat16)
    branch_vel = jnp.einsum("pnd,dc->pnc", final_in, w_final, preferred_element_type=jnp.float32)
    half_width = latent.shape[2]
    branch_index = lax.axis_index("cfg")
    own_half = lax.dynamic_slice_in_dim(branch_vel, branch_index * half_width, half_width, 2)
    other_half = lax.dynamic_slice_in_dim(
        branch_vel, (1 - branch_index) * half_width, half_width, 2
    )
    partner = partner_2(other_half.astype(jnp.bfloat16), "cfg", 0).astype(other_half.dtype)
    first = branch_index == 0
    cond_vel = jnp.where(first, own_half, partner)
    uncond_vel = jnp.where(first, partner, own_half)
    velocity = uncond_vel + 4.5 * (cond_vel - uncond_vel)
    latent_next = latent - 0.04 * velocity
    return (velocity, latent_next)


def solution(mesh):
    placed = (
        P("cfg", "req", "seq", None),
        P("cfg", "req", "seq", None),
        P("cfg", None, None),
        P("cfg", "req"),
        P("req", "seq", "cfg"),
        P(("req", "seq"), None),
        P(None, "seq", None),
        P(None, "seq", None),
        P("seq", None),
        P(("cfg", "req", "seq"), None),
        P(("cfg", "req", "seq"), None),
        P(),
    )
    return jax.shard_map(
        local,
        mesh=mesh,
        in_specs=placed,
        out_specs=(P("req", "seq", "cfg"), P("req", "seq", "cfg")),
        check_vma=False,
    )
```

profile of v0, /device:TPU:0, one launch (start us, length us, event | category | flops | bytes accessed | tf_op | source)
XLA Modules:
  0.0 504.4 jit_solution(12453538248403719071)
XLA Ops:
  8.1 1.6 convolution_bitcast_fusion
  9.6 99.6 %all-gather = f32[64,240,16]{1,2,0:T(8,128)S(1)} all-gather(f32[1,240,16]{1,2,0:T(8,128)S(1)} %convolution_bitcast_fusion), channel_id=1, replica_groups=mesh['cfg'=2,'req'=8,'seq'=8] {'req','seq'}, dimensions={0}, use_global_device_ids=true | all-gather | bytes 998400 | tf_op jit(solution)/shard_map/all_gather | solution.py:49
  109.2 1.6 copy.18
  110.8 2.9 reshape.139
  113.7 1.1 dynamic-slice_bitcast_fusion
  117.4 1.3 fusion.78
  118.8 16.0 %all-gather.9.cloned.1.call-done = bf16[2,192,1536]{2,1,0:T(8,128)(2,1)} async-done(((bf16[2,24,1536]{2,1,0:T(8,128)(2,1)}), bf16[2,192,1536]{2,1,0:T(8,128)(2,1)}) %all-gather.9.cloned.1.call-update) | async-done | bytes 1179664 | tf_op jit(solution)/shard_map/all_gather | solution.py:59
  134.8 2.9 fusion.83
  138.5 39.0 %all-gather.7.cloned.1.call-done = bf16[2,1024,1536]{2,1,0:T(8,128)(2,1)} async-done(((bf16[2,128,1536]{2,1,0:T(8,128)(2,1)}), bf16[2,1024,1536]{2,1,0:T(8,128)(2,1)}) %all-gather.7.cloned.1.call-update) | async-done | bytes 6291472 | tf_op jit(solution)/shard_map/all_gather | solution.py:58
  177.5 6.9 %convert_bitcast_fusion.1 = bf16[3,2,1024,192]{2,3,0,1:T(8,128)(2,1)S(1)} fusion(bf16[2,1024,1536]{2,1,0:T(8,128)(2,1)} %all-gather.7.cloned.1.call-done, bf16[3,192,1536]{2,1,0:T(8,128)(2,1)S(1)} %copy-done), kind=kOutput, calls=%fused_computation.51 | convolution fusion | flops 3625058304 | bytes 10420224 | tf_op jit(solution)/shard_map/pnd,jed->jpne/dot_general | solution.py:61
  184.4 1.4 fusion.117
  185.8 1.5 reshape_squeeze.3
  187.3 2.3 copy.44
  190.6 1.0 pad_maximum_fusion
  191.6 31.2 %while.11 = (s32[]{:T(128)}, bf16[2,2,512,3,64]{2,4,3,1,0:T(8,128)(2,1)}, bf16[2,2,512,3,64]{2,4,3,1,0:T(8,128)(2,1)}, bf16[2,1216,3,64]{1,3,2,0:T(8,128)(2,1)},...) while((s32[]{:T(128)}, bf16[2,2,512,3,64]{2,4,3,1,0:T(8,128)(2,1)}, ...), condition=%wide.region_7.8_spmd.clone, body=%wide.region_4.7_spmd.clone.sunk | while | flops 1468276480 | bytes 4117205 | solution.py:90
  191.7 7.2 %fusion.142 = f32[2,3,512]{2,1,0:T(4,128)} fusion(pred[2,1216]{1,0:T(4,128)(4,1)S(1)} %iota_compare_fusion.2, bf16[2,1216,3,64]{1,3,2,0:T(8,128)(2,1)} %get-tuple-element.143, bf16[2,2,512,3,64]{2,4,3,1,0:T(8,128)(2,1)} %get-tuple-element.142, s32[]{:T(128)} %get-tuple-element.133), kind=kOutput, calls=%fused_computation.138.clone.1 | convolution fusion | flops 493094080 | bytes 1391488 | tf_op jit(solution)/shard_map/while/body/eval_jaxpr/sub | solution.py:85
  198.9 8.3 %fusion.143 = bf16[2,2,512,3,64]{2,4,3,1,0:T(8,128)(2,1)} fusion(bf16[2,2,512,3,64]{2,4,3,1,0:T(8,128)(2,1)} %get-tuple-element.134, s32[]{:T(128)} %get-tuple-element.133, bf16[2,1216,3,64]{1,3,2,0:T(8,128)(2,1)S(1)} %get-tuple-element.144, f32[2,3,512]{2,1,0:T(4,128)} %fusion.142, pred[2,1216]{1,0:T(4,128)(4,1)S(1)} %iota_compare_fusion.2, ...), kind=kOutput, calls=%fused_computation.13.clone.1 | convolution fusion | flops 975179968 | bytes 2723200 | tf_op jit(solution)/shard_map/while/body/eval_jaxpr/phqk,pkhe->pqhe/dot_general | solution.py:86
  207.3 7.2 %fusion.142 = f32[2,3,512]{2,1,0:T(4,128)} fusion(pred[2,1216]{1,0:T(4,128)(4,1)S(1)} %iota_compare_fusion.2, bf16[2,1216,3,64]{1,3,2,0:T(8,128)(2,1)} %get-tuple-element.143, bf16[2,2,512,3,64]{2,4,3,1,0:T(8,128)(2,1)} %get-tuple-element.142, s32[]{:T(128)} %get-tuple-element.133), kind=kOutput, calls=%fused_computation.138.clone.1 | convolution fusion | flops 493094080 | bytes 1391488 | tf_op jit(solution)/shard_map/while/body/eval_jaxpr/sub | solution.py:85
  214.5 8.3 %fusion.143 = bf16[2,2,512,3,64]{2,4,3,1,0:T(8,128)(2,1)} fusion(bf16[2,2,512,3,64]{2,4,3,1,0:T(8,128)(2,1)} %get-tuple-element.134, s32[]{:T(128)} %get-tuple-element.133, bf16[2,1216,3,64]{1,3,2,0:T(8,128)(2,1)S(1)} %get-tuple-element.144, f32[2,3,512]{2,1,0:T(4,128)} %fusion.142, pred[2,1216]{1,0:T(4,128)(4,1)S(1)} %iota_compare_fusion.2, ...), kind=kOutput, calls=%fused_computation.13.clone.1 | convolution fusion | flops 975179968 | bytes 2723200 | tf_op jit(solution)/shard_map/while/body/eval_jaxpr/phqk,pkhe->pqhe/dot_general | solution.py:86
  222.8 2.8 copy.20
  225.7 2.5 reshape.132
  228.2 5.5 %convert_bitcast_fusion = bf16[1024,2,1536]{2,0,1:T(8,128)(2,1)} fusion(bf16[2,1024,192]{1,2,0:T(8,128)(2,1)S(1)} %reshape.132, bf16[192,1536]{1,0:T(8,128)(2,1)} %param.22), kind=kOutput, calls=%fused_computation.41 | convolution fusion | flops 1211105280 | bytes 7667712 | tf_op jit(solution)/shard_map/pnh,hd->npd/dot_general | solution.py:94
  235.0 43.4 %reduce-scatter.3.cloned.1.call-done = bf16[128,2,1536]{2,0,1:T(8,128)(2,1)} async-done(((bf16[1024,2,1536]{2,0,1:T(8,128)(2,1)}), bf16[128,2,1536]{2,0,1:T(8,128)(2,1)}) %reduce-scatter.3.cloned.1.call-update) | async-done | bytes 786448 | tf_op jit(solution)/shard_map/reduce_scatter | solution.py:93
  278.4 1.5 convert_reduce_fusion
  280.3 1.3 fusion.74
  281.7 46.6 %all-gather.13.cloned.1.call-done = bf16[3072,1536]{1,0:T(8,128)(2,1)} async-done(((bf16[48,1536]{1,0:T(8,128)(2,1)}), bf16[3072,1536]{1,0:T(8,128)(2,1)}) %all-gather.13.cloned.1.call-update) | async-done | bytes 9437200 | tf_op jit(solution)/shard_map/all_gather | solution.py:112
  328.3 86.0 %all-gather.15.cloned.1.call-done = bf16[3072,1536]{1,0:T(8,128)(2,1)} async-done(((bf16[48,1536]{1,0:T(8,128)(2,1)}), bf16[3072,1536]{1,0:T(8,128)(2,1)}) %all-gather.15.cloned.1.call-update) | async-done | bytes 9437200 | tf_op jit(solution)/shard_map/all_gather | solution.py:113
  414.3 27.9 %all-gather.11.cloned.1.call-done = bf16[512,1536]{1,0:T(8,128)(2,1)} async-done(((bf16[256,1536]{1,0:T(8,128)(2,1)}), bf16[512,1536]{1,0:T(8,128)(2,1)}) %all-gather.11.cloned.1.call-update) | async-done | bytes 1572880 | tf_op jit(solution)/shard_map/all_gather | solution.py:109
  442.2 18.0 %fusion.57 = bf16[512,1536]{1,0:T(8,128)(2,1)} fusion(bf16[3072,1536]{1,0:T(8,128)(2,1)} %all-gather.15.cloned.1.call-done, bf16[512,1536]{1,0:T(8,128)(2,1)} %all-gather.11.cloned.1.call-done, bf16[3072,1536]{1,0:T(8,128)(2,1)} %all-gather.13.cloned.1.call-done), kind=kOutput, calls=%fused_computation.47 | convolution fusion | flops 9678618624 | bytes 22020096 | tf_op jit(solution)/shard_map/dot_general | solution.py:25
  460.3 29.6 %reduce-scatter.5.cloned.1.call-done = bf16[256,1536]{1,0:T(8,128)(2,1)} async-done(((bf16[512,1536]{1,0:T(8,128)(2,1)}), bf16[256,1536]{1,0:T(8,128)(2,1)}) %reduce-scatter.5.cloned.1.call-update) | async-done | bytes 786448 | tf_op jit(solution)/shard_map/reduce_scatter | solution.py:115
  489.9 1.5 fusion.86
  492.9 3.5 collective-permute-done
  (79 shorter events, 8.4 us)
Async XLA Ops:
  8.0 169.5 %copy-start = (bf16[3,192,1536]{2,1,0:T(8,128)(2,1)S(1)}, bf16[3,192,1536]{2,1,0:T(8,128)(2,1)}, u32[]{:S(2)}) copy-start(bf16[3,192,1536]{2,1,0:T(8,128)(2,1)} %param.20) | copy-start | bytes 5308420
  8.0 126.8 %all-gather.9.cloned.1.call-start = ((), (), s32[]{:S(2)}) async-start(), calls=%async_computation.3 | async-start | bytes 1327104 | tf_op jit(solution)/shard_map/all_gather | solution.py:59
  110.8 4.8 copy-start.5
  110.8 6.0 %copy-start.1 = (bf16[1,2,128,1536]{3,2,1,0:T(8,128)(2,1)S(1)}, bf16[1,2,128,1536]{3,2,1,0:T(8,128)(2,1)}, u32[]{:S(2)}) copy-start(bf16[1,2,128,1536]{3,2,1,0:T(8,128)(2,1)} %param.14) | copy-start | bytes 2359300
  116.7 60.8 %all-gather.7.cloned.1.call-start = ((), (), s32[]{:S(2)}) async-start(), calls=%async_computation.2 | async-start | bytes 7077888 | tf_op jit(solution)/shard_map/all_gather | solution.py:58
  117.0 1.8 copy-start.15
  118.7 159.7 %reduce-scatter.3.cloned.1.call-start = ((), (), s32[]{:S(2)}) async-start(), calls=%async_computation.4 | async-start | bytes 7077888 | tf_op jit(solution)/shard_map/reduce_scatter | solution.py:93
  187.3 2.3 copy-start.3
  187.3 3.3 copy-start.2
  187.3 3.3 copy-start.6
  233.7 1.2 copy-start.8
  233.7 1.3 copy-start.11
  233.7 1.3 copy-start.12
  233.7 94.6 %all-gather.13.cloned.1.call-start = ((), (), s32[]{:S(2)}) async-start(), calls=%async_computation.6 | async-start | bytes 9584640 | tf_op jit(solution)/shard_map/all_gather | solution.py:112
  234.3 180.0 %all-gather.15.cloned.1.call-start = ((), (), s32[]{:S(2)}) async-start(), calls=%async_computation.7 | async-start | bytes 9584640 | tf_op jit(solution)/shard_map/all_gather | solution.py:113
  234.9 207.3 %all-gather.11.cloned.1.call-start = ((), (), s32[]{:S(2)}) async-start(), calls=%async_computation.5 | async-start | bytes 2359296 | tf_op jit(solution)/shard_map/all_gather | solution.py:109
  281.6 178.7 %copy-start.7 = (f32[2,1,1,1536]{3,1,0,2:T(1,128)S(1)}, f32[2,1,1,1536]{3,1,0,2:T(1,128)}, u32[]{:S(2)}) copy-start(f32[2,1,1,1536]{3,1,0,2:T(1,128)} %get-tuple-element.71) | copy-start | bytes 36868
  281.6 178.7 %copy-start.9 = (f32[2,1,1,1536]{3,1,0,2:T(1,128)S(1)}, f32[2,1,1,1536]{3,1,0,2:T(1,128)}, u32[]{:S(2)}) copy-start(f32[2,1,1,1536]{3,1,0,2:T(1,128)} %get-tuple-element.72) | copy-start | bytes 36868
  281.6 178.7 %copy-start.10 = (f32[2,1,1,1536]{3,1,0,2:T(1,128)S(1)}, f32[2,1,1,1536]{3,1,0,2:T(1,128)}, u32[]{:S(2)}) copy-start(f32[2,1,1,1536]{3,1,0,2:T(1,128)} %get-tuple-element.73) | copy-start | bytes 36868
  281.6 208.3 %reduce-scatter.5.cloned.1.call-start = ((), (), s32[]{:S(2)}) async-start(), calls=%async_computation.8 | async-start | bytes 2359296 | tf_op jit(solution)/shard_map/reduce_scatter | solution.py:115
  460.3 31.7 %copy-start.14 = (bf16[1536,64]{0,1:T(8,128)(2,1)S(1)}, bf16[1536,64]{0,1:T(8,128)(2,1)}, u32[]{:S(2)}) copy-start(bf16[1536,64]{0,1:T(8,128)(2,1)} %param.25) | copy-start | bytes 589828
  489.9 1.6 copy-start.4
  491.9 4.5 copy-start.13
  492.6 3.8 collective-permute-start
Sparse Core Ops, SparseCore 0:
  116.8 17.9 all-gather.8
  136.5 40.9 all-gather.6
  233.8 44.5 reduce-scatter.2
Sparse Core Ops, SparseCore 1:
  237.3 91.0 all-gather.12
  331.3 82.9 all-gather.14
  415.8 26.4 all-gather.10
  460.3 29.5 reduce-scatter.4
where the time goes:
time: 505 us; the launch traced here: 504 us
  waiting for transfers between devices  293 us (58%)
  blocking collectives  99.6 us (20%)
  matrix products  66.5 us (13%)
  local copies, waits for them, and re-layouts  17.2 us (3%)
  between operations  15.8 us (3%)
  other arithmetic  11.6 us (2%)
    all_gather x1, blocking collectives, local(): mod_all = lax.all_gather(mod_part, ('req', 'seq'), axis=1, tiled=True)  99.6 us
    all_gather x1, waiting for transfers between devices, local(): lax.all_gather(w_down, ('req', 'seq'), axis=0, tiled=True)  86 us
    all_gather x1, waiting for transfers between devices, local(): lax.all_gather(w_up, ('req', 'seq'), axis=0, tiled=True)  46.6 us
    reduce_scatter x1, waiting for transfers between devices, local(): lax.psum_scatter(jnp.einsum('pnh,hd->npd', attended, w_attn_out, preferre...  43.4 us
    all_gather x1, waiting for transfers between devices, local(): lax.all_gather(a_img, 'seq', axis=1, tiled=True)  39 us
    reduce_scatter x1, waiting for transfers between devices, local(): lax.psum_scatter(partial_out.astype(jnp.bfloat16), 'cfg', scatter_dimensi...  29.6 us
    all_gather x1, waiting for transfers between devices, local(): both = lax.all_gather(own_rows, 'cfg', axis=0, tiled=True)  27.9 us
    dot_general x1, matrix products, mlp_term(): return jnp.dot(hidden, down_block, preferred_element_type=jnp.float32)  18 us
  transfers between devices with their start and end apart: 8, of which 8 were waited for; matrix products, arithmetic and copies ran while one was open for 2% of the time, Pallas kernels for 0%

commit v1 on v0

--- a/solution.py
+++ b/solution.py
@@ -4,6 +4,29 @@
 from jax.sharding import PartitionSpec as P
 
 HEAD = 64
+
+
+def prepare_the_desk(sheet, chip_axis):
+    r2 = jax.lax.axis_size(chip_axis)
+    p_next = jax.lax.axis_index(chip_axis)
+    spare, mat_out, later = (r2, p_next, sheet.shape[1])
+    pieces_in = tuple(((dd, (dd + 1) % spare) for dd in range(spare)))
+    copies = tuple(((dd, (dd - 1) % spare) for dd in range(spare)))
+    wide_out = jnp.zeros((*sheet.shape[:1], spare * later, *sheet.shape[2:]), sheet.dtype)
+    wide_out = lax.dynamic_update_slice_in_dim(wide_out, sheet, mat_out * later, axis=1)
+    state_next = u_next = sheet
+    o_now = spare // 2
+    for nth in range(1, o_now + 1):
+        state_next = jax.lax.ppermute(state_next, axis_name=chip_axis, perm=pieces_in)
+        wide_out = lax.dynamic_update_slice_in_dim(
+            wide_out, state_next, (mat_out - nth) % spare * later, axis=1
+        )
+        if nth < spare - o_now:
+            u_next = jax.lax.ppermute(u_next, axis_name=chip_axis, perm=copies)
+            wide_out = lax.dynamic_update_slice_in_dim(
+                wide_out, u_next, (mat_out + nth) % spare * later, axis=1
+            )
+    return wide_out
 
 
 def partner_2(shard, axis, apart):
@@ -56,7 +79,7 @@
     ).astype(jnp.bfloat16)
     full_img, full_txt = (
         lax.all_gather(a_img, "seq", axis=1, tiled=True),
-        lax.all_gather(a_txt, "seq", axis=1, tiled=True),
+        prepare_the_desk(a_txt, chip_axis="seq"),
     )
     proj_img = jnp.einsum(
         "pnd,jed->jpne", full_img, w_qkv_img, preferred_element_type=jnp.float32

time: 505 us -> 482 us (0.954)
  waiting for transfers between devices: 293 us -> 255 us
  starting transfers between devices: 0.63 us -> 10.6 us
  local copies, waits for them, and re-layouts: 17.2 us -> 23.3 us
    all_gather x1, waiting for transfers between devices: 39 us -> 2.06 us  [local(): lax.all_gather(a_img, 'seq', axis=1, tiled=True)]
    ppermute x0 -> x7, waiting for transfers between devices: none -> 18.4 us  [the longest x4 9.65 us: prepare_the_desk(): jax.lax.ppermute(state_next, axis_name=chip_axis, perm=pieces_in)]
    all_gather x1 -> x0, waiting for transfers between devices: 16 us -> none  [local(): lax.all_gather(a_txt, 'seq', axis=1, tiled=True)]
    ppermute x0 -> x7, starting transfers between devices: none -> 10 us  [the longest x3 9.64 us: prepare_the_desk(): u_next = jax.lax.ppermute(u_next, axis_name=chip_axis, perm=copies)]
  transfers between devices with their start and end apart: 8 -> 14, of which waited for: 8 -> 14; matrix products, arithmetic and copies ran while one was open for 2% -> 2% of each run, Pallas kernels for 0% -> 0%
where the time goes in v1:
time: 482 us; the launch traced here: 481 us
  waiting for transfers between devices  255 us (53%)
  blocking collectives  99.6 us (21%)
  matrix products  66 us (14%)
  local copies, waits for them, and re-layouts  23.3 us (5%)
  between operations  15.9 us (3%)
  other arithmetic  11 us (2%)
  starting transfers between devices  10.6 us (2%)
    all_gather x1, blocking collectives, local(): mod_all = lax.all_gather(mod_part, ('req', 'seq'), axis=1, tiled=True)  99.6 us
    all_gather x1, waiting for transfers between devices, local(): lax.all_gather(w_down, ('req', 'seq'), axis=0, tiled=True)  86 us
    all_gather x1, waiting for transfers between devices, local(): lax.all_gather(w_up, ('req', 'seq'), axis=0, tiled=True)  46.7 us
    reduce_scatter x1, waiting for transfers between devices, local(): lax.psum_scatter(jnp.einsum('pnh,hd->npd', attended, w_attn_out, preferre...  40.3 us
    reduce_scatter x1, waiting for transfers between devices, local(): lax.psum_scatter(partial_out.astype(jnp.bfloat16), 'cfg', scatter_dimensi...  28.9 us
    all_gather x1, waiting for transfers between devices, local(): both = lax.all_gather(own_rows, 'cfg', axis=0, tiled=True)  27.9 us
    dot_general x1, matrix products, mlp_term(): return jnp.dot(hidden, down_block, preferred_element_type=jnp.float32)  18 us
    dot_general x2, matrix products, attend(): jnp.einsum('phqk,pkhe->pqhe', probs, value_heads, preferred_element_type=...  16.6 us
  transfers between devices with their start and end apart: 14, of which 14 were waited for; matrix products, arithmetic and copies ran while one was open for 2% of the time, Pallas kernels for 0%

profile of v1, /device:TPU:0, one launch (start us, length us, event | category | flops | bytes accessed | tf_op | source)
XLA Modules:
  0.0 481.3 jit_solution(11907795216637875949)
XLA Ops:
  8.1 1.6 convolution_bitcast_fusion
  9.6 99.6 %all-gather = f32[64,240,16]{1,2,0:T(8,128)S(1)} all-gather(f32[1,240,16]{1,2,0:T(8,128)S(1)} %convolution_bitcast_fusion), channel_id=1, replica_groups=mesh['cfg'=2,'req'=8,'seq'=8] {'req','seq'}, dimensions={0}, use_global_device_ids=true | all-gather | bytes 998400 | tf_op jit(solution)/shard_map/all_gather | solution.py:72
  109.2 1.6 copy.18
  110.8 1.9 reshape.139
  119.1 2.6 collective-permute-start.1
  121.7 2.8 collective-permute-done
  124.5 2.8 collective-permute-done.1
  127.2 3.5 collective-permute-start.3
  133.4 3.2 collective-permute-done.3
  136.6 3.5 collective-permute-start.5
  143.0 2.9 collective-permute-done.5
  146.5 4.7 collective-permute-done.6
  151.9 2.4 fusion.83
  155.1 2.1 all-gather.6.cloned.1.call-done
  157.2 6.8 %convert_bitcast_fusion.1 = bf16[3,2,1024,192]{2,3,0,1:T(8,128)(2,1)S(1)} fusion(bf16[2,1024,1536]{2,1,0:T(8,128)(2,1)} %all-gather.6.cloned.1.call-done, bf16[3,192,1536]{2,1,0:T(8,128)(2,1)S(1)} %copy-done), kind=kOutput, calls=%fused_computation.51 | convolution fusion | flops 3625058304 | bytes 10420224 | tf_op jit(solution)/shard_map/pnd,jed->jpne/dot_general | solution.py:84
  167.0 2.3 copy.44
  171.3 31.2 %while.11 = (s32[]{:T(128)}, bf16[2,2,512,3,64]{2,4,3,1,0:T(8,128)(2,1)}, bf16[2,2,512,3,64]{2,4,3,1,0:T(8,128)(2,1)}, bf16[2,1216,3,64]{1,3,2,0:T(8,128)(2,1)},...) while((s32[]{:T(128)}, bf16[2,2,512,3,64]{2,4,3,1,0:T(8,128)(2,1)}, ...), condition=%wide.region_7.8_spmd.clone, body=%wide.region_4.7_spmd.clone.sunk | while | flops 1468276480 | bytes 4117205 | solution.py:113
  171.4 7.2 %fusion.143 = f32[2,3,512]{2,1,0:T(4,128)} fusion(pred[2,1216]{1,0:T(4,128)(4,1)S(1)} %iota_compare_fusion.2, bf16[2,1216,3,64]{1,3,2,0:T(8,128)(2,1)} %get-tuple-element.145, bf16[2,2,512,3,64]{2,4,3,1,0:T(8,128)(2,1)} %get-tuple-element.144, s32[]{:T(128)} %get-tuple-element.135), kind=kOutput, calls=%fused_computation.146.clone.1 | convolution fusion | flops 493094080 | bytes 1391488 | tf_op jit(solution)/shard_map/while/body/eval_jaxpr/sub | solution.py:108
  178.6 8.3 %fusion.144 = bf16[2,2,512,3,64]{2,4,3,1,0:T(8,128)(2,1)} fusion(bf16[2,2,512,3,64]{2,4,3,1,0:T(8,128)(2,1)} %get-tuple-element.136, s32[]{:T(128)} %get-tuple-element.135, bf16[2,1216,3,64]{1,3,2,0:T(8,128)(2,1)S(1)} %get-tuple-element.146, f32[2,3,512]{2,1,0:T(4,128)} %fusion.143, pred[2,1216]{1,0:T(4,128)(4,1)S(1)} %iota_compare_fusion.2, ...), kind=kOutput, calls=%fused_computation.13.clone.1 | convolution fusion | flops 975179968 | bytes 2723200 | tf_op jit(solution)/shard_map/while/body/eval_jaxpr/phqk,pkhe->pqhe/dot_general | solution.py:109
  187.0 7.2 %fusion.143 = f32[2,3,512]{2,1,0:T(4,128)} fusion(pred[2,1216]{1,0:T(4,128)(4,1)S(1)} %iota_compare_fusion.2, bf16[2,1216,3,64]{1,3,2,0:T(8,128)(2,1)} %get-tuple-element.145, bf16[2,2,512,3,64]{2,4,3,1,0:T(8,128)(2,1)} %get-tuple-element.144, s32[]{:T(128)} %get-tuple-element.135), kind=kOutput, calls=%fused_computation.146.clone.1 | convolution fusion | flops 493094080 | bytes 1391488 | tf_op jit(solution)/shard_map/while/body/eval_jaxpr/sub | solution.py:108
  194.2 8.3 %fusion.144 = bf16[2,2,512,3,64]{2,4,3,1,0:T(8,128)(2,1)} fusion(bf16[2,2,512,3,64]{2,4,3,1,0:T(8,128)(2,1)} %get-tuple-element.136, s32[]{:T(128)} %get-tuple-element.135, bf16[2,1216,3,64]{1,3,2,0:T(8,128)(2,1)S(1)} %get-tuple-element.146, f32[2,3,512]{2,1,0:T(4,128)} %fusion.143, pred[2,1216]{1,0:T(4,128)(4,1)S(1)} %iota_compare_fusion.2, ...), kind=kOutput, calls=%fused_computation.13.clone.1 | convolution fusion | flops 975179968 | bytes 2723200 | tf_op jit(solution)/shard_map/while/body/eval_jaxpr/phqk,pkhe->pqhe/dot_general | solution.py:109
  202.5 2.8 copy.20
  205.4 2.5 reshape.132
  207.9 5.5 %convert_bitcast_fusion = bf16[1024,2,1536]{2,0,1:T(8,128)(2,1)} fusion(bf16[2,1024,192]{1,2,0:T(8,128)(2,1)S(1)} %reshape.132, bf16[192,1536]{1,0:T(8,128)(2,1)} %param.22), kind=kOutput, calls=%fused_computation.41 | convolution fusion | flops 1211105280 | bytes 7667712 | tf_op jit(solution)/shard_map/pnh,hd->npd/dot_general | solution.py:117
  214.8 40.3 %reduce-scatter.3.cloned.1.call-done = bf16[128,2,1536]{2,0,1:T(8,128)(2,1)} async-done(((bf16[1024,2,1536]{2,0,1:T(8,128)(2,1)}), bf16[128,2,1536]{2,0,1:T(8,128)(2,1)}) %reduce-scatter.3.cloned.1.call-update) | async-done | bytes 786448 | tf_op jit(solution)/shard_map/reduce_scatter | solution.py:116
  258.3 46.7 %all-gather.10.cloned.1.call-done = bf16[3072,1536]{1,0:T(8,128)(2,1)} async-done(((bf16[48,1536]{1,0:T(8,128)(2,1)}), bf16[3072,1536]{1,0:T(8,128)(2,1)}) %all-gather.10.cloned.1.call-update) | async-done | bytes 9437200 | tf_op jit(solution)/shard_map/all_gather | solution.py:135
  305.0 86.0 %all-gather.12.cloned.1.call-done = bf16[3072,1536]{1,0:T(8,128)(2,1)} async-done(((bf16[48,1536]{1,0:T(8,128)(2,1)}), bf16[3072,1536]{1,0:T(8,128)(2,1)}) %all-gather.12.cloned.1.call-update) | async-done | bytes 9437200 | tf_op jit(solution)/shard_map/all_gather | solution.py:136
  390.9 27.9 %all-gather.8.cloned.1.call-done = bf16[512,1536]{1,0:T(8,128)(2,1)} async-done(((bf16[256,1536]{1,0:T(8,128)(2,1)}), bf16[512,1536]{1,0:T(8,128)(2,1)}) %all-gather.8.cloned.1.call-update) | async-done | bytes 1572880 | tf_op jit(solution)/shard_map/all_gather | solution.py:132
  418.9 18.0 %fusion.57 = bf16[512,1536]{1,0:T(8,128)(2,1)} fusion(bf16[3072,1536]{1,0:T(8,128)(2,1)} %all-gather.12.cloned.1.call-done, bf16[512,1536]{1,0:T(8,128)(2,1)} %all-gather.8.cloned.1.call-done, bf16[3072,1536]{1,0:T(8,128)(2,1)} %all-gather.10.cloned.1.call-done), kind=kOutput, calls=%fused_computation.47 | convolution fusion | flops 9678618624 | bytes 22020096 | tf_op jit(solution)/shard_map/dot_general | solution.py:48
  437.6 28.9 %reduce-scatter.5.cloned.1.call-done = bf16[256,1536]{1,0:T(8,128)(2,1)} async-done(((bf16[512,1536]{1,0:T(8,128)(2,1)}), bf16[256,1536]{1,0:T(8,128)(2,1)}) %reduce-scatter.5.cloned.1.call-update) | async-done | bytes 786448 | tf_op jit(solution)/shard_map/reduce_scatter | solution.py:138
  466.5 1.6 fusion.86
  469.6 3.5 collective-permute-done.7
  (102 shorter events, 26.4 us)
Async XLA Ops:
  8.0 149.2 %copy-start = (bf16[3,192,1536]{2,1,0:T(8,128)(2,1)S(1)}, bf16[3,192,1536]{2,1,0:T(8,128)(2,1)}, u32[]{:S(2)}) copy-start(bf16[3,192,1536]{2,1,0:T(8,128)(2,1)} %param.20) | copy-start | bytes 5308420
  8.0 149.2 %all-gather.6.cloned.1.call-start = ((), (), s32[]{:S(2)}) async-start(), calls=%async_computation.2 | async-start | bytes 7077888 | tf_op jit(solution)/shard_map/all_gather | solution.py:81
  110.8 4.3 copy-start.1
  115.3 1.8 copy-start.5
  117.0 4.6 copy-start.17
  117.0 138.0 %reduce-scatter.3.cloned.1.call-start = ((), (), s32[]{:S(2)}) async-start(), calls=%async_computation.3 | async-start | bytes 7077888 | tf_op jit(solution)/shard_map/reduce_scatter | solution.py:116
  117.7 1.0 copy-start.6
  118.7 5.8 %collective-permute-start = (bf16[2,24,1536]{2,1,0:T(8,128)(2,1)S(1)}, bf16[2,24,1536]{2,1,0:T(8,128)(2,1)S(1)}, u32[]{:S(2)}, u32[]{:S(2)}) collective-permute-start(bf16[2,24,1536]{2,1,0:T(8,128)(2,1)S(1)} %get-tuple-element.67), channel_id=1, source_target_pairs={{0,1},{1,2},{2,3},{3,4},{4,5},{5,6},{6,7},{7,0},{8,9},{9,10},{10,1... | collective-permute-start | bytes 442376 | tf_op jit(solution)/shard_map/ppermute | solution.py:20
  119.1 8.2 %collective-permute-start.1 = (bf16[2,24,1536]{2,1,0:T(8,128)(2,1)S(1)}, bf16[2,24,1536]{2,1,0:T(8,128)(2,1)S(1)}, u32[]{:S(2)}, u32[]{:S(2)}) collective-permute-start(bf16[2,24,1536]{2,1,0:T(8,128)(2,1)S(1)} %get-tuple-element.67), channel_id=1, source_target_pairs={{0,7},{1,0},{2,1},{3,2},{4,3},{5,4},{6,5},{7,6},{8,15},{9,8},{10,9... | collective-permute-start | bytes 442376 | tf_op jit(solution)/shard_map/ppermute | solution.py:25
  121.7 30.2 %copy-start.15 = (bf16[3,192,1536]{2,1,0:T(8,128)(2,1)S(1)}, bf16[3,192,1536]{2,1,0:T(8,128)(2,1)}, u32[]{:S(2)}) copy-start(bf16[3,192,1536]{2,1,0:T(8,128)(2,1)} %param.21) | copy-start | bytes 5308420
  124.5 8.9 %collective-permute-start.2 = (bf16[2,24,1536]{2,1,0:T(8,128)(2,1)S(1)}, bf16[2,24,1536]{2,1,0:T(8,128)(2,1)S(1)}, u32[]{:S(2)}, u32[]{:S(2)}) collective-permute-start(bf16[2,24,1536]{2,1,0:T(8,128)(2,1)S(1)} %collective-permute-done), channel_id=1, source_target_pairs={{0,1},{1,2},{2,3},{3,4},{4,5},{5,6},{6,7},{7,0},{8,9},{9,10},{10,1... | collective-permute-start | bytes 442376 | tf_op jit(solution)/shard_map/ppermute | solution.py:20
  127.2 9.3 %collective-permute-start.3 = (bf16[2,24,1536]{2,1,0:T(8,128)(2,1)S(1)}, bf16[2,24,1536]{2,1,0:T(8,128)(2,1)S(1)}, u32[]{:S(2)}, u32[]{:S(2)}) collective-permute-start(bf16[2,24,1536]{2,1,0:T(8,128)(2,1)S(1)} %collective-permute-done.1), channel_id=1, source_target_pairs={{0,7},{1,0},{2,1},{3,2},{4,3},{5,4},{6,5},{7,6},{8,15},{9,8},{10,9... | collective-permute-start | bytes 442376 | tf_op jit(solution)/shard_map/ppermute | solution.py:25
  133.4 8.9 %collective-permute-start.4 = (bf16[2,24,1536]{2,1,0:T(8,128)(2,1)S(1)}, bf16[2,24,1536]{2,1,0:T(8,128)(2,1)S(1)}, u32[]{:S(2)}, u32[]{:S(2)}) collective-permute-start(bf16[2,24,1536]{2,1,0:T(8,128)(2,1)S(1)} %collective-permute-done.2), channel_id=1, source_target_pairs={{0,1},{1,2},{2,3},{3,4},{4,5},{5,6},{6,7},{7,0},{8,9},{9,10},{10,1... | collective-permute-start | bytes 442376 | tf_op jit(solution)/shard_map/ppermute | solution.py:20
  136.6 9.3 %collective-permute-start.5 = (bf16[2,24,1536]{2,1,0:T(8,128)(2,1)S(1)}, bf16[2,24,1536]{2,1,0:T(8,128)(2,1)S(1)}, u32[]{:S(2)}, u32[]{:S(2)}) collective-permute-start(bf16[2,24,1536]{2,1,0:T(8,128)(2,1)S(1)} %collective-permute-done.3), channel_id=1, source_target_pairs={{0,7},{1,0},{2,1},{3,2},{4,3},{5,4},{6,5},{7,6},{8,15},{9,8},{10,9... | collective-permute-start | bytes 442376 | tf_op jit(solution)/shard_map/ppermute | solution.py:25
  142.3 8.9 %collective-permute-start.6 = (bf16[2,24,1536]{2,1,0:T(8,128)(2,1)S(1)}, bf16[2,24,1536]{2,1,0:T(8,128)(2,1)S(1)}, u32[]{:S(2)}, u32[]{:S(2)}) collective-permute-start(bf16[2,24,1536]{2,1,0:T(8,128)(2,1)S(1)} %collective-permute-done.4), channel_id=1, source_target_pairs={{0,1},{1,2},{2,3},{3,4},{4,5},{5,6},{6,7},{7,0},{8,9},{9,10},{10,1... | collective-permute-start | bytes 442376 | tf_op jit(solution)/shard_map/ppermute | solution.py:20
  167.0 2.3 copy-start.3
  167.0 3.3 copy-start.2
  167.0 3.3 copy-start.7
  213.4 1.2 copy-start.9
  213.4 1.3 copy-start.12
  213.4 1.3 copy-start.13
  213.5 91.5 %all-gather.10.cloned.1.call-start = ((), (), s32[]{:S(2)}) async-start(), calls=%async_computation.5 | async-start | bytes 9584640 | tf_op jit(solution)/shard_map/all_gather | solution.py:135
  214.0 176.9 %all-gather.12.cloned.1.call-start = ((), (), s32[]{:S(2)}) async-start(), calls=%async_computation.6 | async-start | bytes 9584640 | tf_op jit(solution)/shard_map/all_gather | solution.py:136
  214.6 204.2 %all-gather.8.cloned.1.call-start = ((), (), s32[]{:S(2)}) async-start(), calls=%async_computation.4 | async-start | bytes 2359296 | tf_op jit(solution)/shard_map/all_gather | solution.py:132
  258.3 208.3 %reduce-scatter.5.cloned.1.call-start = ((), (), s32[]{:S(2)}) async-start(), calls=%async_computation.7 | async-start | bytes 2359296 | tf_op jit(solution)/shard_map/reduce_scatter | solution.py:138
  436.9 0.7 copy-start.8
  436.9 0.7 copy-start.10
  436.9 0.7 copy-start.11
  466.5 1.6 copy-start.4
  466.5 2.0 copy-start.16
  468.6 4.5 copy-start.14
  469.2 3.8 collective-permute-start.7
Sparse Core Ops, SparseCore 0:
  117.2 39.9 all-gather.5
  213.6 41.4 reduce-scatter.2
Sparse Core Ops, SparseCore 1:
  217.0 87.9 all-gather.9
  307.9 82.9 all-gather.11
  392.4 26.4 all-gather.7
  437.0 29.5 reduce-scatter.4
